TPU v7x, 32 devices: a whole 2x2x4 slice. The times are simulated.
32 devices in a mesh: groups: 2 (over y), replica: 4 (over z), tensor: 4 (over x, core).
Axes of the slice: x: 2, y: 2, z: 4, core: 2. Of those that a mesh axis runs over, the one named last changes fastest.
Arguments:
- queries: bfloat16 [144, 8192], P(('groups', 'replica'), 'tensor'), parts along dimension 0, may hold values from -64 to 64
- past_cache: bfloat16 [2, 144, 128, 1024], P(None, ('groups', 'replica'), None, 'tensor'), parts along dimension 1, may hold values from -6 to 6
- lengths: int32 [144], P(('groups', 'replica')), parts along dimension 0, may hold values from 2 to 128, as said below
- live_counts: int32 [8], P(('groups', 'replica')), parts along dimension 0, may hold values from 1 to 16, as said below
- adapter_index: int32 [144], P(('groups', 'replica')), parts along dimension 0, may hold values from 0 to 15, as said below
- adapter_down: bfloat16 [16, 16, 8192], P('replica', None, 'tensor'), may hold values from -0.0625 to 0.0625
- adapter_up: bfloat16 [16, 16, 8192], P('replica', None, 'tensor'), may hold values from -6 to 6
Outputs:
- attention: bfloat16 [144, 8192], P(('groups', 'replica'), 'tensor'), parts along dimension 0
- adapted: bfloat16 [144, 8192], P(('groups', 'replica'), 'tensor'), parts along dimension 0
There are 2 independent parts, one for each index of `groups`. A program takes and returns all parts, laid end to end along the dimension named above; an argument that names none is the same for every part. Nothing has to cross between parts.
Inputs may be any that keep to these rules, and one draw needn't show every extreme that they name: `adapter_index`: over the first 16 slots of all replicas, exactly 4 distinct adapters appear, homed on 4 distinct replicas. Each of the last 2 slots of a replica names an adapter outside that set; the homes (adapter a lives on replica a // 4) of one replica's last 2 slots are distinct, and some replica is the home of one such slot of every replica. `lengths`: some request has exactly 128. `live_counts`: some replica has exactly 16.
All inputs are finite; a program needn't handle non-finite values.
Results may differ from a plain program's by a relative error of at most 0.008.
Values may be sent and summed in bfloat16 or wider, within the bound.
A program may use at most 64 MiB of HBM per device.

v0:
```python
import math

import jax
import jax.numpy as jnp
from jax import lax
from jax.sharding import PartitionSpec as P

HEAD_DIM = 128
STAY = 16


SCALING = 2.0


def broadcast(block, axis, owner):
    block = jnp.where(lax.axis_index(axis) == owner, block, jnp.zeros_like(block))
    return lax.psum(block, axis)


def attend(queries, keys, values, visible):
    count = queries.shape[0]
    key_width = keys.shape[-1]
    key_heads = key_width // HEAD_DIM
    group_size = queries.shape[1] // key_width
    context = keys.shape[1]
    query_rows = queries.reshape(count, key_heads, group_size, HEAD_DIM)
    key_rows = keys.reshape(count, context, key_heads, HEAD_DIM)
    value_rows = values.reshape(count, context, key_heads, HEAD_DIM)
    scores = jnp.einsum(
        "nhgd,nlhd->nhgl", query_rows, key_rows, preferred_element_type=jnp.float32
    ) / math.sqrt(HEAD_DIM)
    scores = jnp.where(visible[:, None, None, :], scores, -jnp.inf)
    peak = jnp.max(scores, axis=-1, keepdims=True)
    raised = jnp.exp(scores - peak)
    weights = (raised / jnp.sum(raised, axis=-1, keepdims=True)).astype(jnp.bfloat16)
    mixed = jnp.einsum("nhgl,nlhd->nhgd", weights, value_rows, preferred_element_type=jnp.float32)
    return mixed.reshape(count, key_heads * group_size * HEAD_DIM)


def widen_rows(rank_rows, up_rows):
    widened = jnp.einsum("nr,nrc->nc", rank_rows, up_rows.astype(jnp.float32))
    return (SCALING * widened).astype(jnp.bfloat16)


def on_device(queries, past_cache, lengths, live_counts, adapter_index, adapter_down, adapter_up):
    slots = queries.shape[0]
    moving = slots - STAY
    replicas = lax.axis_size("replica")
    hot_total = min(8, replicas)
    local_count = adapter_down.shape[0]
    total_adapters = local_count * replicas
    context = past_cache.shape[2]
    position = jnp.arange(context, dtype=jnp.int32)
    slot_index = jnp.arange(slots, dtype=jnp.int32)
    alive = (slot_index >= STAY) | (slot_index < live_counts[0])
    visible = position[None, :] < lengths[:, None]
    stay_index = adapter_index[:STAY]
    catalog = jnp.arange(total_adapters, dtype=jnp.int32)
    usage = jnp.sum((stay_index[:, None] == catalog[None, :]).astype(jnp.int32), axis=0)
    usage = lax.psum(usage, "replica")
    ranking = jnp.where(usage > 0, total_adapters - catalog, 0)
    hot_index = total_adapters - lax.top_k(ranking, hot_total)[0]
    down_list = []
    up_list = []
    for hot_slot in range(hot_total):
        holder = hot_index[hot_slot] // local_count
        within = hot_index[hot_slot] % local_count
        local_pair = (
            lax.dynamic_index_in_dim(adapter_down, within, 0, False),
            lax.dynamic_index_in_dim(adapter_up, within, 0, False),
        )
        fetched = (
            broadcast(local_pair[0], "replica", holder),
            broadcast(local_pair[1], "replica", holder),
        )
        down_list.append(fetched[0])
        up_list.append(fetched[1])
    hot_down = jnp.stack(down_list)
    hot_up = jnp.stack(up_list)
    hot_pick = (stay_index[:, None] == hot_index[None, :]).astype(jnp.bfloat16)
    stay_down = jnp.einsum("nh,hrc->nrc", hot_pick, hot_down)
    stay_up = jnp.einsum("nh,hrc->nrc", hot_pick, hot_up)
    stay_attention = attend(
        queries[:STAY], past_cache[0, :STAY], past_cache[1, :STAY], visible[:STAY]
    )
    stay_attention = jnp.where(alive[:STAY, None], stay_attention, 0.0).astype(jnp.bfloat16)
    stay_partial = jnp.einsum(
        "nc,nrc->nr", stay_attention, stay_down, preferred_element_type=jnp.float32
    )
    moved_index = adapter_index[STAY:]
    homes = moved_index // local_count
    replica_ids = jnp.arange(replicas, dtype=jnp.int32)
    matched = homes[None, :] == replica_ids[:, None]
    occupied = jnp.any(matched, axis=1)
    source_slot = jnp.sum(
        jnp.where(matched, jnp.arange(moving, dtype=jnp.int32)[None, :], 0), axis=1
    )
    wanted = jnp.where(occupied, jnp.take(moved_index, source_slot) % local_count, -1)
    local_catalog = jnp.arange(local_count, dtype=jnp.int32)
    chooser = (
        lax.all_to_all(wanted[:, None], "replica", split_axis=0, concat_axis=0, tiled=True)[
            :, :, None
        ]
        == local_catalog[None, None, :]
    ).astype(jnp.bfloat16)
    send_down = jnp.einsum("sna,arc->snrc", chooser, adapter_down)
    send_up = jnp.einsum("sna,arc->snrc", chooser, adapter_up)
    got_down = lax.all_to_all(send_down, "replica", split_axis=0, concat_axis=0, tiled=True)
    got_up = lax.all_to_all(send_up, "replica", split_axis=0, concat_axis=0, tiled=True)
    moved_down = jnp.take(got_down[:, 0], homes, axis=0)
    moved_up = jnp.take(got_up[:, 0], homes, axis=0)
    moved_attention = attend(
        queries[STAY:], past_cache[0, STAY:], past_cache[1, STAY:], visible[STAY:]
    ).astype(jnp.bfloat16)
    moved_partial = jnp.einsum(
        "nc,nrc->nr", moved_attention, moved_down, preferred_element_type=jnp.float32
    )
    rank_rows = lax.psum(jnp.concatenate([stay_partial, moved_partial], axis=0), "tensor")
    stay_adapted = widen_rows(rank_rows[:STAY], stay_up)
    moved_adapted = widen_rows(rank_rows[STAY:], moved_up)
    attention = jnp.concatenate([stay_attention, moved_attention], axis=0)
    adapted = jnp.concatenate([stay_adapted, moved_adapted], axis=0)
    return (attention, adapted)


def solution(mesh):
    in_specs = (
        P(("groups", "replica"), "tensor"),
        P(None, ("groups", "replica"), None, "tensor"),
        P(("groups", "replica")),
        P(("groups", "replica")),
        P(("groups", "replica")),
        P("replica", None, "tensor"),
        P("replica", None, "tensor"),
    )
    out_specs = (P(("groups", "replica"), "tensor"), P(("groups", "replica"), "tensor"))
    return jax.shard_map(
        on_device, mesh=mesh, in_specs=in_specs, out_specs=out_specs, check_vma=False
    )
```

profile of v0, /device:TPU:0, one launch (start us, length us, event | category | flops | bytes accessed | tf_op | source)
XLA Modules:
  0.0 125.1 jit_solution(2885234638877340328)
XLA Ops:
  7.2 0.7 compare_and_fusion
  7.9 0.7 slice.70
  8.8 0.6 gather_fusion
  9.5 0.7 copy.78
  10.1 6.3 %all-to-all-start = ((s32[4,1,1]{2,1,0:T(1,128)}), s32[4,1,1]{2,1,0:T(1,128)S(1)}, u32[]{:S(2)}, u32[]{:S(2)}) async-start(s32[4,1,1]{2,1,0:T(1,128)} %copy.78), calls=%async_computation | async-start | bytes 4096 | tf_op jit(solution)/shard_map/all_to_all | solution.py:101
  16.5 0.7 convert_reduce_fusion
  17.2 8.8 %psum.70 = s32[16]{0:T(128)S(1)} all-reduce(s32[16]{0:T(128)S(1)} %convert_reduce_fusion), channel_id=1, replica_groups=mesh['groups'=2,'replica'=4,'tensor'=4] {'replica'}, use_global_device_ids=true, to_apply=%region_5.6 | all-reduce | flops 16 | bytes 128 | tf_op jit(solution)/shard_map/psum | solution.py:60
  26.1 1.2 top_k.9
  27.3 0.7 fusion.67
  38.2 1.2 copy.73
  39.4 1.2 copy.81
  40.6 1.4 %broadcast_select_fusion.7 = (bf16[1,16,2048]{2,0,1:T(2,128)(2,1)}, bf16[1,16,2048]{2,0,1:T(2,128)(2,1)}, bf16[1,16,2048]{2,0,1:T(2,128)(2,1)}, bf16[1,16,2048]{2,0,1:T(2,128)(2,1)}) fusion(pred[]{:T(512)S(6)} %eq.87, bf16[4,16,2048]{2,0,1:T(4,128)(2,1)S(1)} %copy.73, s32[]{:T(128)S(6)} %select_n.215, s32[]{:T(128)S(6)} %select_n.233, pred[]{:T(512)S(6)} %eq.90, ...), kind=kLoop, calls=%fused_computation.43 | loop fusion | flops 131072 | bytes 524308 | tf_op jit(solution)/shard_map/jit(_where)/select_n | solution.py:16
  42.0 1.5 %broadcast_select_fusion.6 = (bf16[1,16,2048]{2,0,1:T(2,128)(2,1)}, bf16[1,16,2048]{2,0,1:T(2,128)(2,1)}, bf16[1,16,2048]{2,0,1:T(2,128)(2,1)}, bf16[1,16,2048]{2,0,1:T(2,128)(2,1)}) fusion(pred[]{:T(512)S(6)} %eq.87, bf16[4,16,2048]{2,0,1:T(4,128)(2,1)S(1)} %copy.81, s32[]{:T(128)S(6)} %select_n.215, s32[]{:T(128)S(6)} %select_n.233, pred[]{:T(512)S(6)} %eq.90, ...), kind=kLoop, calls=%fused_computation.42 | loop fusion | flops 131072 | bytes 524308 | tf_op jit(solution)/shard_map/jit(_where)/select_n | solution.py:16
  43.5 1.0 fusion.66
  44.6 1.7 %fusion.65 = (bf16[1,16,128,256]{3,2,1,0:T(8,128)(2,1)S(1)}, bf16[1,16,128,256]{3,2,1,0:T(8,128)(2,1)S(1)}) fusion(bf16[2,18,128,256]{3,2,1,0:T(8,128)(2,1)} %param.10), kind=kLoop, calls=%fused_computation.114 | loop fusion | bytes 4194304 | tf_op jit(solution)/shard_map/slice | solution.py:84
  47.2 1.3 %copy.103 = bf16[1,16,128,256]{2,3,1,0:T(8,128)(2,1)} copy(bf16[1,16,128,256]{3,2,1,0:T(8,128)(2,1)S(1)} %get-tuple-element.17) | data formatting | bytes 2097152
  48.6 0.7 copy.102
  50.5 1.9 %fusion.37 = bf16[16,2,8,128]{3,2,1,0:T(8,128)(2,1)S(1)} fusion(bf16[16,128,2,128]{1,3,2,0:T(8,128)(2,1)} %bitcast.99, f32[16,2,8]{2,1,0:T(2,128)S(1)} %fusion.69, f32[16,2,8,128]{3,2,1,0:T(8,128)S(1)} %fusion.4), kind=kOutput, calls=%fused_computation.58 | convolution fusion | flops 8487295 | bytes 1246208 | tf_op jit(solution)/shard_map/nhgl,nlhd->nhgd/dot_general | solution.py:36
  53.1 0.8 copy.80
  53.9 3.4 %all-to-all-start.1 = ((bf16[4,1,16,2048]{3,2,1,0:T(8,128)(2,1)}), bf16[4,1,16,2048]{3,2,1,0:T(8,128)(2,1)S(1)}, u32[]{:S(2)}, u32[]{:S(2)}) async-start(bf16[4,1,16,2048]{3,2,1,0:T(8,128)(2,1)} %copy.80), calls=%async_computation.1 | async-start | bytes 524288 | tf_op jit(solution)/shard_map/all_to_all | solution.py:108
  57.7 0.8 copy.86
  58.6 14.4 %all-to-all-done.1 = bf16[4,1,16,2048]{3,2,1,0:T(8,128)(2,1)S(1)} async-done(((bf16[4,1,16,2048]{3,2,1,0:T(8,128)(2,1)}), bf16[4,1,16,2048]{3,2,1,0:T(8,128)(2,1)S(1)}, u32[]{:S(2)}, u32[]{:S(2)}) %all-to-all-start.1) | async-done | bytes 262176 | tf_op jit(solution)/shard_map/all_to_all | solution.py:108
  72.9 3.4 %all-to-all-start.2 = ((bf16[4,1,16,2048]{3,2,1,0:T(8,128)(2,1)}), bf16[4,1,16,2048]{3,2,1,0:T(8,128)(2,1)S(1)}, u32[]{:S(2)}, u32[]{:S(2)}) async-start(bf16[4,1,16,2048]{3,2,1,0:T(8,128)(2,1)} %copy.86), calls=%async_computation.2 | async-start | bytes 524288 | tf_op jit(solution)/shard_map/all_to_all | solution.py:109
  76.4 0.6 gather_fusion.1
  77.0 6.2 %all-to-all-done.2 = bf16[4,1,16,2048]{3,2,1,0:T(8,128)(2,1)S(1)} async-done(((bf16[4,1,16,2048]{3,2,1,0:T(8,128)(2,1)}), bf16[4,1,16,2048]{3,2,1,0:T(8,128)(2,1)S(1)}, u32[]{:S(2)}, u32[]{:S(2)}) %all-to-all-start.2) | async-done | bytes 262176 | tf_op jit(solution)/shard_map/all_to_all | solution.py:109
  83.9 17.2 %all-reduce.3.cloned.1.call-done = (bf16[1,16,2048]{2,0,1:T(2,128)(2,1)}, bf16[1,16,2048]{2,0,1:T(2,128)(2,1)}, bf16[1,16,2048]{2,0,1:T(2,128)(2,1)}, bf16[1,16,...) async-done(((bf16[1,16,2048]{2,0,1:T(2,128)(2,1)}, ...) | async-done | bytes 524304 | tf_op jit(solution)/shard_map/psum | solution.py:17
  101.2 2.1 %fusion.12 = bf16[16,16,2048]{2,0,1:T(8,128)(2,1)S(1)} fusion(bf16[1,16,2048]{2,0,1:T(2,128)(2,1)} %get-tuple-element.6, bf16[1,16,2048]{2,0,1:T(2,128)(2,1)} %get-tuple-element.7, bf16[1,16,2048]{2,0,1:T(2,128)(2,1)} %get-tuple-element.8, bf16[1,16,2048]{2,0,1:T(2,128)(2,1)} %get-tuple-element.9, s32[16]{0:T(128)S(1)} %bitcast.116, ...), kind=kOutput, calls=%fused_computation.20 | convolution fusion | flops 5242944 | bytes 1310800 | tf_op jit(solution)/shard_map/nh,hrc->nrc/dot_general | solution.py:81
  103.3 0.7 fusion.10
  104.0 11.1 %psum.75 = f32[18,16]{1,0:T(8,128)S(1)} all-reduce(f32[18,16]{1,0:T(8,128)S(1)} %pad_maximum_fusion.2), channel_id=1, replica_groups=mesh['groups'=2,'replica'=4,'tensor'=4] {'tensor'}, use_global_device_ids=true, to_apply=%region_13.15 | all-reduce | flops 288 | bytes 2304 | tf_op jit(solution)/shard_map/psum | solution.py:118
  115.4 0.9 fusion.20
  116.3 1.2 fusion.8
  117.6 0.7 pad_maximum_fusion
  (56 shorter events, 3.9 us)
Async XLA Ops:
  10.1 42.4 %all-to-all-start = ((s32[4,1,1]{2,1,0:T(1,128)}), s32[4,1,1]{2,1,0:T(1,128)S(1)}, u32[]{:S(2)}, u32[]{:S(2)}) async-start(s32[4,1,1]{2,1,0:T(1,128)} %copy.78), calls=%async_computation | async-start | bytes 4096 | tf_op jit(solution)/shard_map/all_to_all | solution.py:101
  16.5 84.6 %all-reduce.3.cloned.1.call-start = ((), (), s32[]{:S(2)}) async-start(), calls=%async_computation.3 | async-start | bytes 2097152 | tf_op jit(solution)/shard_map/psum | solution.py:17
  43.5 2.7 %copy-start = (bf16[18,2048]{1,0:T(8,128)(2,1)S(1)}, bf16[18,2048]{1,0:T(8,128)(2,1)}, u32[]{:S(2)}) copy-start(bf16[18,2048]{1,0:T(8,128)(2,1)} %param.9) | copy-start | bytes 221188
  43.5 2.8 %copy-start.1 = (s32[18]{0:T(128)S(1)}, s32[18]{0:T(128)}, u32[]{:S(2)}) copy-start(s32[18]{0:T(128)} %param.11) | copy-start | bytes 220
  52.4 48.7 %copy-start.6 = (s32[18]{0:T(128)S(1)}, s32[18]{0:T(128)}, u32[]{:S(2)}) copy-start(s32[18]{0:T(128)} %param.13) | copy-start | bytes 220
  53.9 19.0 %all-to-all-start.1 = ((bf16[4,1,16,2048]{3,2,1,0:T(8,128)(2,1)}), bf16[4,1,16,2048]{3,2,1,0:T(8,128)(2,1)S(1)}, u32[]{:S(2)}, u32[]{:S(2)}) async-start(bf16[4,1,16,2048]{3,2,1,0:T(8,128)(2,1)} %copy.80), calls=%async_computation.1 | async-start | bytes 524288 | tf_op jit(solution)/shard_map/all_to_all | solution.py:108
  72.9 10.2 %all-to-all-start.2 = ((bf16[4,1,16,2048]{3,2,1,0:T(8,128)(2,1)}), bf16[4,1,16,2048]{3,2,1,0:T(8,128)(2,1)S(1)}, u32[]{:S(2)}, u32[]{:S(2)}) async-start(bf16[4,1,16,2048]{3,2,1,0:T(8,128)(2,1)} %copy.86), calls=%async_computation.2 | async-start | bytes 524288 | tf_op jit(solution)/shard_map/all_to_all | solution.py:109
  101.1 14.2 %copy-start.2 = (bf16[1,16,2048]{2,0,1:T(2,128)(2,1)S(1)}, bf16[1,16,2048]{2,0,1:T(2,128)(2,1)}, u32[]{:S(2)}) copy-start(bf16[1,16,2048]{2,0,1:T(2,128)(2,1)} %get-tuple-element.10) | copy-start | bytes 196612
  101.1 14.2 %copy-start.3 = (bf16[1,16,2048]{2,0,1:T(2,128)(2,1)S(1)}, bf16[1,16,2048]{2,0,1:T(2,128)(2,1)}, u32[]{:S(2)}) copy-start(bf16[1,16,2048]{2,0,1:T(2,128)(2,1)} %get-tuple-element.11) | copy-start | bytes 196612
  101.1 14.2 %copy-start.4 = (bf16[1,16,2048]{2,0,1:T(2,128)(2,1)S(1)}, bf16[1,16,2048]{2,0,1:T(2,128)(2,1)}, u32[]{:S(2)}) copy-start(bf16[1,16,2048]{2,0,1:T(2,128)(2,1)} %get-tuple-element.12) | copy-start | bytes 196612
  101.1 14.2 %copy-start.5 = (bf16[1,16,2048]{2,0,1:T(2,128)(2,1)S(1)}, bf16[1,16,2048]{2,0,1:T(2,128)(2,1)}, u32[]{:S(2)}) copy-start(bf16[1,16,2048]{2,0,1:T(2,128)(2,1)} %get-tuple-element.13) | copy-start | bytes 196612
Sparse Core Ops, SparseCore 0:
  43.6 57.4 all-reduce.2
where the time goes:
time: 126 us; the launch traced here: 125 us
  waiting for transfers between devices  37.8 us (30%)
  between operations  25.2 us (20%)
  blocking collectives  19.9 us (16%)
  starting transfers between devices  13.2 us (10%)
  local copies, waits for them, and re-layouts  12.9 us (10%)
  matrix products  8.78 us (7%)
  other arithmetic  7.4 us (6%)
    psum x1, waiting for transfers between devices, broadcast(): return lax.psum(block, axis)  17.2 us
    all_to_all x1, waiting for transfers between devices, on_device(): lax.all_to_all(send_down, 'replica', split_axis=0, concat_axis=0, tiled=T...  14.4 us
    psum x1, blocking collectives, on_device(): lax.psum(jnp.concatenate([stay_partial, moved_partial], axis=0), 'tensor')  11.1 us
    psum x1, blocking collectives, on_device(): usage = lax.psum(usage, 'replica')  8.8 us
    all_to_all x1, starting transfers between devices, on_device(): lax.all_to_all(wanted[:, None], 'replica', split_axis=0, concat_axis=0, t...  6.35 us
    all_to_all x1, waiting for transfers between devices, on_device(): lax.all_to_all(send_up, 'replica', split_axis=0, concat_axis=0, tiled=True)  6.15 us
    unnamed x24, local copies, waits for them, and re-layouts  4.62 us
    all_to_all x1, starting transfers between devices, on_device(): lax.all_to_all(send_up, 'replica', split_axis=0, concat_axis=0, tiled=True)  3.4 us
  transfers between devices with their start and end apart: 4, of which 3 were waited for; matrix products, arithmetic and copies ran while one was open for 16% of the time, Pallas kernels for 0%

commit v1 on v0

v1 whole, which is shorter than its diff:
```python
import functools
import math

import jax
import jax.numpy as jnp
from jax import lax
from jax.experimental import pallas as pl
from jax.experimental.pallas import tpu as pltpu
from jax.sharding import PartitionSpec as P

HEAD_DIM = 128
STAY = 16
SCALING = 2.0
GROUP = 4
MESH = pl.DeviceIdType.MESH
F32 = jnp.float32
BF16 = jnp.bfloat16


def dot_nt(a, b):
    return lax.dot_general(a, b, (((1,), (1,)), ((), ())), preferred_element_type=F32)


def dot_nn(a, b):
    return lax.dot_general(a, b, (((1,), (0,)), ((), ())), preferred_element_type=F32)


def widen(ranks, up):
    high = ranks.astype(BF16)
    low = (ranks - high.astype(F32)).astype(BF16)
    return SCALING * (dot_nn(high, up) + dot_nn(low, up))


def kernel(
    replicas, tensors,
    lengths, live, index, queries, cache, down, up,
    attention, adapted,
    q_in, kv, down_v, up_v, q_rows, o_rows,
    idx_buf, row_out, row_in, row_send, row_back, hot_down, hot_up, rank_m, rank_s,
    local_sem, group_sem,
    idx_s, idx_r, row_s, row_r, back_s, back_r, hd_s, hd_r, hu_s, hu_r, tm_s, tm_r, ts_s, ts_r,
):
    me = lax.axis_index("replica")
    mine = lax.axis_index("tensor")
    slots, cols = queries.shape
    moving = slots - STAY
    context = cache.shape[2]
    key_heads = cache.shape[3] // HEAD_DIM
    heads = cols // HEAD_DIM
    size = heads // key_heads
    count, rank = down.shape[0], down.shape[1]
    groups = STAY // GROUP

    def peer(offset):
        return {"replica": lax.rem(me + offset, replicas)}

    def side(offset):
        return {"tensor": lax.rem(mine + offset, tensors)}

    barrier = pltpu.get_barrier_semaphore()
    for d in range(1, replicas):
        pl.semaphore_signal(barrier, inc=1, device_id=peer(d), device_id_type=MESH)
    for d in range(1, tensors):
        pl.semaphore_signal(barrier, inc=1, device_id=side(d), device_id_type=MESH)

    load_q = pltpu.make_async_copy(queries, q_in, local_sem.at[0])
    load_m = pltpu.make_async_copy(
        cache.at[:, pl.ds(STAY, moving)], kv.at[:, pl.ds(STAY, moving)], local_sem.at[1]
    )
    load_d = pltpu.make_async_copy(down, down_v, local_sem.at[2])
    load_u = pltpu.make_async_copy(up, up_v, local_sem.at[3])
    loads = [
        pltpu.make_async_copy(
            cache.at[:, pl.ds(g * GROUP, GROUP)], kv.at[:, pl.ds(g * GROUP, GROUP)], group_sem.at[g]
        )
        for g in range(groups)
    ]
    load_q.start()
    load_m.start()
    for copy in loads[:2]:
        copy.start()
    load_d.start()
    load_u.start()
    for copy in loads[2:]:
        copy.start()

    def to_peers(source, target, send, recv):
        return [
            pltpu.make_async_remote_copy(
                src_ref=source(d), dst_ref=target.at[d], send_sem=send.at[d - 1],
                recv_sem=recv.at[d - 1], device_id=peer(d), device_id_type=MESH,
            )
            for d in range(1, replicas)
        ]

    def to_sides(buffer, send, recv):
        return [
            pltpu.make_async_remote_copy(
                src_ref=buffer.at[0], dst_ref=buffer.at[d], send_sem=send.at[d - 1],
                recv_sem=recv.at[d - 1], device_id=side(d), device_id_type=MESH,
            )
            for d in range(1, tensors)
        ]

    send_idx = to_peers(lambda d: idx_buf.at[0], idx_buf, idx_s, idx_r)
    send_rows = to_peers(lambda d: row_out.at[d], row_in, row_s, row_r)
    send_hd = to_peers(lambda d: hot_down.at[0], hot_down, hd_s, hd_r)
    send_hu = to_peers(lambda d: hot_up.at[0], hot_up, hu_s, hu_r)
    send_back = [
        pltpu.make_async_remote_copy(
            src_ref=row_send.at[d], dst_ref=row_back.at[d], send_sem=back_s.at[d - 1],
            recv_sem=back_r.at[d - 1], device_id=peer(replicas - d), device_id_type=MESH,
        )
        for d in range(1, replicas)
    ]
    send_tm = to_sides(rank_m, tm_s, tm_r)
    send_ts = to_sides(rank_s, ts_s, ts_r)

    lane = lax.broadcasted_iota(jnp.int32, (1, 128), 1)
    line = jnp.full((1, 128), -1, jnp.int32)
    for i in range(slots):
        line = jnp.where(lane == i, index[i], line)
    idx_buf[0] = line
    stay_row = lax.broadcasted_iota(jnp.int32, (STAY, 1), 0)
    stay_rel = jnp.zeros((STAY, 1), jnp.int32)
    for i in range(STAY):
        stay_rel = jnp.where(stay_row == i, lax.rem(me - index[i] // count + replicas, replicas), stay_rel)
    move_rel = [lax.rem(index[STAY + j] // count - me + replicas, replicas) for j in range(moving)]

    load_q.wait()
    for h in range(heads):
        q_rows[pl.ds(h, slots, stride=heads), :] = q_in[:, h * HEAD_DIM:(h + 1) * HEAD_DIM].astype(F32)

    head_row = lax.broadcasted_iota(jnp.int32, (heads, 1), 0) // size
    position = lax.broadcasted_iota(jnp.int32, (1, context), 1)

    def attend(requests):
        for n in requests:
            q = q_rows[n * heads:(n + 1) * heads, :]
            wide = jnp.concatenate(
                [jnp.where(head_row == g, q, 0.0) for g in range(key_heads)], axis=1
            ).astype(BF16)
            scores = dot_nt(wide, kv[0, n]) / math.sqrt(HEAD_DIM)
            scores = jnp.where(position < lengths[n], scores, -jnp.inf)
            peak = jnp.max(scores, axis=-1, keepdims=True)
            raised = jnp.exp(scores - peak)
            weights = (raised / jnp.sum(raised, axis=-1, keepdims=True)).astype(BF16)
            mixed = dot_nn(weights, kv[1, n])
            out = jnp.zeros((heads, HEAD_DIM), F32)
            for g in range(key_heads):
                out = jnp.where(head_row == g, mixed[:, g * HEAD_DIM:(g + 1) * HEAD_DIM], out)
            o_rows[n * heads:(n + 1) * heads, :] = out

    def gather_rows(first, number):
        return jnp.concatenate(
            [o_rows[pl.ds(first * heads + h, number, stride=heads), :] for h in range(heads)], axis=1
        )

    load_m.wait()
    attend(range(STAY, slots))
    moved = gather_rows(STAY, moving).astype(BF16)
    attention[STAY:slots, :] = moved
    moved = moved.astype(F32)
    replica_row = lax.broadcasted_iota(jnp.int32, (replicas, 1), 0)
    picked = jnp.zeros((replicas, cols), F32)
    for j in range(moving):
        picked = jnp.where(replica_row == move_rel[j], moved[j:j + 1, :], picked)
    row_in[0] = picked[0:1, :]
    for d in range(1, replicas):
        row_out[d] = picked[d:d + 1, :]

    pl.semaphore_wait(barrier, replicas - 1 + tensors - 1)
    for copy in send_idx:
        copy.start()
    for copy in send_rows:
        copy.start()

    for g in range(groups // 2):
        loads[g].wait()
        attend(range(g * GROUP, (g + 1) * GROUP))

    load_d.wait()
    load_u.wait()
    for copy in send_idx:
        copy.wait_recv()
    table = jnp.concatenate([idx_buf[d] for d in range(replicas)], axis=0)
    here = (table >= 0) & (table // count == me)
    local = jnp.where(here, table - me * count, -1)
    lanes = lax.broadcasted_iota(jnp.int32, table.shape, 1)
    hot = jnp.maximum(jnp.max(jnp.where(lanes < STAY, local, -1)), 0)
    hot_down[0] = down_v[hot]
    hot_up[0] = up_v[hot]
    for copy in send_hd:
        copy.start()
    for copy in send_hu:
        copy.start()

    asked = jnp.max(jnp.where(lanes >= STAY, local, -1), axis=1, keepdims=True)
    for copy in send_rows:
        copy.wait_recv()
    rows = jnp.concatenate([row_in[d] for d in range(replicas)], axis=0).astype(BF16)
    partial = dot_nt(rows, down_v[...].reshape(count * rank, cols))
    owner = lax.broadcasted_iota(jnp.int32, partial.shape, 1) // rank
    rank_m[0] = jnp.where(owner == asked, partial, 0.0)
    for copy in send_tm:
        copy.start()

    for g in range(groups // 2, groups):
        loads[g].wait()
        attend(range(g * GROUP, (g + 1) * GROUP))

    for copy in send_tm:
        copy.wait_recv()
    total = rank_m[0]
    for d in range(1, tensors):
        total = total + rank_m[d]
    made = widen(total, up_v[...].reshape(count * rank, cols)).astype(BF16).astype(F32)
    row_back[0] = made[0:1, :]
    for d in range(1, replicas):
        row_send[d] = made[d:d + 1, :]
    for copy in send_back:
        copy.start()

    stay = jnp.where(stay_row < live[0], gather_rows(0, STAY), 0.0).astype(BF16)
    attention[0:STAY, :] = stay

    for copy in send_hd:
        copy.wait_recv()
    partial = dot_nt(stay, hot_down[...].reshape(replicas * rank, cols))
    owner = lax.broadcasted_iota(jnp.int32, partial.shape, 1) // rank
    rank_s[0] = jnp.where(owner == stay_rel, partial, 0.0)
    for copy in send_ts:
        copy.start()

    for copy in send_back:
        copy.wait_recv()
    back = jnp.concatenate([row_back[d] for d in range(replicas)], axis=0)
    adapted[STAY:slots, :] = jnp.concatenate(
        [
            jnp.sum(jnp.where(replica_row == move_rel[j], back, 0.0), axis=0, keepdims=True)
            for j in range(moving)
        ],
        axis=0,
    ).astype(BF16)

    for copy in send_ts:
        copy.wait_recv()
    total = rank_s[0]
    for d in range(1, tensors):
        total = total + rank_s[d]
    for copy in send_hu:
        copy.wait_recv()
    adapted[0:STAY, :] = widen(total, hot_up[...].reshape(replicas * rank, cols)).astype(BF16)

    for copy in send_idx + send_rows + send_hd + send_hu + send_back + send_tm + send_ts:
        copy.wait_send()


def on_device(replicas, tensors, queries, past_cache, lengths, live_counts, adapter_index, adapter_down, adapter_up):
    slots, cols = queries.shape
    count, rank = adapter_down.shape[0], adapter_down.shape[1]
    heads = cols // HEAD_DIM
    out = jax.ShapeDtypeStruct((slots, cols), BF16)
    smem = pl.BlockSpec(memory_space=pltpu.SMEM)
    anywhere = pl.BlockSpec(memory_space=pl.ANY)
    vmem = pl.BlockSpec(memory_space=pltpu.VMEM)
    dma = pltpu.SemaphoreType.DMA
    rep = dma((max(replicas - 1, 1),))
    ten = dma((max(tensors - 1, 1),))
    scratch = [
        pltpu.VMEM((slots, cols), BF16),
        pltpu.VMEM(past_cache.shape, BF16),
        pltpu.VMEM(adapter_down.shape, BF16),
        pltpu.VMEM(adapter_up.shape, BF16),
        pltpu.VMEM((slots * heads, HEAD_DIM), F32),
        pltpu.VMEM((slots * heads, HEAD_DIM), F32),
        pltpu.VMEM((replicas, 1, 128), jnp.int32),
        pltpu.VMEM((replicas, 1, cols), F32),
        pltpu.VMEM((replicas, 1, cols), F32),
        pltpu.VMEM((replicas, 1, cols), F32),
        pltpu.VMEM((replicas, 1, cols), F32),
        pltpu.VMEM((replicas, rank, cols), BF16),
        pltpu.VMEM((replicas, rank, cols), BF16),
        pltpu.VMEM((tensors, replicas, count * rank), F32),
        pltpu.VMEM((tensors, STAY, replicas * rank), F32),
        dma((4,)),
        dma((STAY // GROUP,)),
        rep, rep, rep, rep, rep, rep, rep, rep, rep, rep, ten, ten, ten, ten,
    ]
    return pl.pallas_call(
        functools.partial(kernel, replicas, tensors),
        out_shape=(out, out),
        in_specs=[smem, smem, smem, anywhere, anywhere, anywhere, anywhere],
        out_specs=(vmem, vmem),
        scratch_shapes=scratch,
        compiler_params=pltpu.CompilerParams(collective_id=0, has_side_effects=True),
    )(lengths, live_counts, adapter_index, queries, past_cache, adapter_down, adapter_up)


def solution(mesh):
    in_specs = (
        P(("groups", "replica"), "tensor"),
        P(None, ("groups", "replica"), None, "tensor"),
        P(("groups", "replica")),
        P(("groups", "replica")),
        P(("groups", "replica")),
        P("replica", None, "tensor"),
        P("replica", None, "tensor"),
    )
    out_specs = (P(("groups", "replica"), "tensor"), P(("groups", "replica"), "tensor"))
    body = functools.partial(on_device, mesh.shape["replica"], mesh.shape["tensor"])
    return jax.shard_map(body, mesh=mesh, in_specs=in_specs, out_specs=out_specs, check_vma=False)
```

time: 126 us -> 28.3 us (0.22)
  waiting for transfers between devices: 37.8 us -> 0 us
  between operations: 25.2 us -> 1.29 us
  Pallas kernels: 0 us -> 23.7 us
  blocking collectives: 19.9 us -> 0 us
  starting transfers between devices: 13.2 us -> 0 us
  local copies, waits for them, and re-layouts: 12.9 us -> 3.08 us
  matrix products: 8.78 us -> 0 us
  other arithmetic: 7.4 us -> 0 us
    pallas_call x0 -> x1, Pallas kernels: none -> 23.7 us  [on_device(): pl.pallas_call(functools.partial(kernel, replicas, tensors), out_shape=(o...]
    all_to_all x3 -> x0, waiting for transfers between devices: 20.5 us -> none  [the longest x1 14.4 us: on_device(): lax.all_to_all(send_down, 'replica', split_axis=0, concat_axis=0, tiled=T...]
    psum x2 -> x0, blocking collectives: 19.9 us -> none  [the longest x1 11.1 us: on_device(): lax.psum(jnp.concatenate([stay_partial, moved_partial], axis=0), 'tensor')]
    psum x1 -> x0, waiting for transfers between devices: 17.2 us -> none  [broadcast(): return lax.psum(block, axis)]
    all_to_all x3 -> x0, starting transfers between devices: 13.2 us -> none  [the longest x1 6.35 us: on_device(): lax.all_to_all(wanted[:, None], 'replica', split_axis=0, concat_axis=0, t...]
    dot_general x12 -> x0, matrix products: 8.78 us -> none  [the longest x2 2.15 us: attend(): jnp.einsum('nhgl,nlhd->nhgd', weights, value_rows, preferred_element_type...]
    slice x8 -> x0, local copies, waits for them, and re-layouts: 4.11 us -> none  [the longest x1 1.68 us: on_device(): past_cache[0, :STAY]]
    select_n x6 -> x0, other arithmetic: 2.92 us -> none  [the longest x2 2.89 us: broadcast(): jnp.where(lax.axis_index(axis) == owner, block, jnp.zeros_like(block))]
  transfers between devices with their start and end apart: 4 -> 0, of which waited for: 3 -> 0; matrix products, arithmetic and copies ran while one was open for 16% -> 0% of each run, Pallas kernels for 0% -> 0%
where the time goes in v1:
time: 28.3 us; the launch traced here: 28.1 us
  Pallas kernels  23.7 us (84%)
  local copies, waits for them, and re-layouts  3.08 us (11%)
  between operations  1.29 us (5%)
    pallas_call x1, Pallas kernels, on_device(): pl.pallas_call(functools.partial(kernel, replicas, tensors), out_shape=(o...  23.7 us
    unnamed x2, local copies, waits for them, and re-layouts  3.08 us

profile of v1, /device:TPU:0, one launch (start us, length us, event | category | flops | bytes accessed | tf_op | source)
XLA Modules:
  0.0 28.1 jit_solution(9284424210444889390)
XLA Ops:
  1.3 23.7 %shard_map.86 = (bf16[18,2048]{1,0:T(8,128)(2,1)}, bf16[18,2048]{1,0:T(8,128)(2,1)}) custom-call(s32[18]{0:T(128)} %lengths.1, s32[1]{0:T(128)S(6)} %copy.11.live, s32[18]{0:T(128)} %index.1, bf16[18,2048]{1,0:T(8,128)(2,1)} %queries.1, bf16[2,18,128,256]{3,2,1,0:T(8,128)(2,1)} %cache.1, bf16[4,16,2048]{2,1,0:T(8,128)(2,1)} %down.1, bf16[4,16,2048]{2,1,0:T(8,128)(2,1)} %up.1), custom_call_target="tpu_custom_call" | custom-call | tf_op jit(solution)/shard_map/pallas_call | solution.py:290
  25.0 1.5 %copy.12 = bf16[18,2048]{1,0:T(8,128)(2,1)} copy(bf16[18,2048]{1,0:T(8,128)(2,1)} %get-tuple-element.4) | data formatting | bytes 147456
  26.5 1.5 %copy.13 = bf16[18,2048]{1,0:T(8,128)(2,1)} copy(bf16[18,2048]{1,0:T(8,128)(2,1)} %get-tuple-element.5) | data formatting | bytes 147456

commit v2 on v1

--- a/solution.py
+++ b/solution.py
@@ -12,6 +12,8 @@
 STAY = 16
 SCALING = 2.0
 GROUP = 4
+REACH = 2
+LIMIT = 67043328 - 240 * 1024
 MESH = pl.DeviceIdType.MESH
 F32 = jnp.float32
 BF16 = jnp.bfloat16
@@ -106,6 +108,56 @@
     send_rows = to_peers(lambda d: row_out.at[d], row_in, row_s, row_r)
     send_hd = to_peers(lambda d: hot_down.at[0], hot_down, hd_s, hd_r)
     send_hu = to_peers(lambda d: hot_up.at[0], hot_up, hu_s, hu_r)
+
+    def straight(d):
+        return ((me + d < replicas) & (d <= REACH)) | ((me + d >= replicas) & (replicas - d <= REACH))
+
+    def onward(buffer, send, recv):
+        steps = {}
+        for d in range(1, replicas):
+            options = []
+            if d >= REACH and d + 1 < replicas:
+                options.append(((me >= d) & (me + 1 < replicas), 1, d + 1, replicas - 1))
+            if replicas - d >= REACH and d > 1:
+                options.append(((me < d) & (me >= 1), replicas - 1, d - 1, 2 * (replicas - 1)))
+            steps[d] = [
+                (flag, pltpu.make_async_remote_copy(
+                    src_ref=buffer.at[d], dst_ref=buffer.at[slot], send_sem=send.at[base + d - 1],
+                    recv_sem=recv.at[slot - 1], device_id=peer(step), device_id_type=MESH,
+                ))
+                for flag, step, slot, base in options
+            ]
+        return steps
+
+    pass_hd = onward(hot_down, hd_s, hd_r)
+    pass_hu = onward(hot_up, hu_s, hu_r)
+    order = sorted(range(1, replicas), key=lambda d: (not pass_hd[d], d))
+
+    def start_if(flag, copy):
+        @pl.when(flag)
+        def _():
+            copy.start()
+
+    def sent_if(flag, copy):
+        @pl.when(flag)
+        def _():
+            copy.wait_send()
+
+    def spread(sends):
+        for d in order:
+            start_if(straight(d), sends[d - 1])
+
+    def relay(sends, passes):
+        for d in order:
+            if passes[d]:
+                sends[d - 1].wait_recv()
+                for flag, copy in passes[d]:
+                    start_if(flag, copy)
+
+    def settle(sends, passes):
+        for d in order:
+            if not passes[d]:
+                sends[d - 1].wait_recv()
     send_back = [
         pltpu.make_async_remote_copy(
             src_ref=row_send.at[d], dst_ref=row_back.at[d], send_sem=back_s.at[d - 1],
@@ -190,10 +242,7 @@
     hot = jnp.maximum(jnp.max(jnp.where(lanes < STAY, local, -1)), 0)
     hot_down[0] = down_v[hot]
     hot_up[0] = up_v[hot]
-    for copy in send_hd:
-        copy.start()
-    for copy in send_hu:
-        copy.start()
+    spread(send_hd)
 
     asked = jnp.max(jnp.where(lanes >= STAY, local, -1), axis=1, keepdims=True)
     for copy in send_rows:
@@ -205,9 +254,13 @@
     for copy in send_tm:
         copy.start()
 
-    for g in range(groups // 2, groups):
+    middle = (groups // 2 + groups) // 2
+    for g in range(groups // 2, middle):
         loads[g].wait()
         attend(range(g * GROUP, (g + 1) * GROUP))
+
+    relay(send_hd, pass_hd)
+    spread(send_hu)
 
     for copy in send_tm:
         copy.wait_recv()
@@ -221,17 +274,20 @@
     for copy in send_back:
         copy.start()
 
+    for g in range(middle, groups):
+        loads[g].wait()
+        attend(range(g * GROUP, (g + 1) * GROUP))
     stay = jnp.where(stay_row < live[0], gather_rows(0, STAY), 0.0).astype(BF16)
     attention[0:STAY, :] = stay
 
-    for copy in send_hd:
-        copy.wait_recv()
+    settle(send_hd, pass_hd)
     partial = dot_nt(stay, hot_down[...].reshape(replicas * rank, cols))
     owner = lax.broadcasted_iota(jnp.int32, partial.shape, 1) // rank
     rank_s[0] = jnp.where(owner == stay_rel, partial, 0.0)
     for copy in send_ts:
         copy.start()
 
+    relay(send_hu, pass_hu)
     for copy in send_back:
         copy.wait_recv()
     back = jnp.concatenate([row_back[d] for d in range(replicas)], axis=0)
@@ -248,12 +304,25 @@
     total = rank_s[0]
     for d in range(1, tensors):
         total = total + rank_s[d]
-    for copy in send_hu:
-        copy.wait_recv()
+    settle(send_hu, pass_hu)
     adapted[0:STAY, :] = widen(total, hot_up[...].reshape(replicas * rank, cols)).astype(BF16)
 
-    for copy in send_idx + send_rows + send_hd + send_hu + send_back + send_tm + send_ts:
+    for copy in send_idx + send_rows + send_back + send_tm + send_ts:
         copy.wait_send()
+    for d in order:
+        for copies, passes in ((send_hd, pass_hd), (send_hu, pass_hu)):
+            sent_if(straight(d), copies[d - 1])
+            for flag, copy in passes[d]:
+                sent_if(flag, copy)
+
+
+def hand_over(attention, adapted, attention_out, adapted_out, sem):
+    first = pltpu.make_async_copy(attention, attention_out, sem.at[0])
+    second = pltpu.make_async_copy(adapted, adapted_out, sem.at[1])
+    first.start()
+    second.start()
+    first.wait()
+    second.wait()
 
 
 def on_device(replicas, tensors, queries, past_cache, lengths, live_counts, adapter_index, adapter_down, adapter_up):
@@ -261,12 +330,14 @@
     count, rank = adapter_down.shape[0], adapter_down.shape[1]
     heads = cols // HEAD_DIM
     out = jax.ShapeDtypeStruct((slots, cols), BF16)
+    held = pltpu.VMEM((slots, cols), BF16)
     smem = pl.BlockSpec(memory_space=pltpu.SMEM)
     anywhere = pl.BlockSpec(memory_space=pl.ANY)
     vmem = pl.BlockSpec(memory_space=pltpu.VMEM)
     dma = pltpu.SemaphoreType.DMA
     rep = dma((max(replicas - 1, 1),))
     ten = dma((max(tensors - 1, 1),))
+    three = dma((max(3 * (replicas - 1), 1),))
     scratch = [
         pltpu.VMEM((slots, cols), BF16),
         pltpu.VMEM(past_cache.shape, BF16),
@@ -285,16 +356,24 @@
         pltpu.VMEM((tensors, STAY, replicas * rank), F32),
         dma((4,)),
         dma((STAY // GROUP,)),
-        rep, rep, rep, rep, rep, rep, rep, rep, rep, rep, ten, ten, ten, ten,
+        rep, rep, rep, rep, rep, rep, three, rep, three, rep, ten, ten, ten, ten,
     ]
-    return pl.pallas_call(
+    results = pl.pallas_call(
         functools.partial(kernel, replicas, tensors),
-        out_shape=(out, out),
+        out_shape=(held, held),
         in_specs=[smem, smem, smem, anywhere, anywhere, anywhere, anywhere],
         out_specs=(vmem, vmem),
         scratch_shapes=scratch,
-        compiler_params=pltpu.CompilerParams(collective_id=0, has_side_effects=True),
+        compiler_params=pltpu.CompilerParams(collective_id=0, has_side_effects=True, vmem_limit_bytes=LIMIT),
     )(lengths, live_counts, adapter_index, queries, past_cache, adapter_down, adapter_up)
+    return pl.pallas_call(
+        hand_over,
+        out_shape=(out, out),
+        in_specs=[vmem, vmem],
+        out_specs=(anywhere, anywhere),
+        scratch_shapes=[dma((2,))],
+        compiler_params=pltpu.CompilerParams(vmem_limit_bytes=4 * 1024 * 1024),
+    )(*results)
 
 
 def solution(mesh):

time: 28.3 us -> 24 us (0.85)
  local copies, waits for them, and re-layouts: 3.08 us -> 0 us
  Pallas kernels: 23.7 us -> 22.5 us
    unnamed x2 -> x0, local copies, waits for them, and re-layouts: 3.08 us -> none
    pallas_call x1 -> x2, Pallas kernels: 23.7 us -> 22.5 us  [the longest x1 21.9 us: on_device(): pl.pallas_call(functools.partial(kernel, replicas, tensors), out_shape=(h...]
where the time goes in v2:
time: 24 us; the launch traced here: 23.8 us
  Pallas kernels  22.5 us (94%)
  between operations  1.29 us (5%)
    pallas_call x1, Pallas kernels, on_device(): pl.pallas_call(functools.partial(kernel, replicas, tensors), out_shape=(h...  21.9 us
    pallas_call x1, Pallas kernels, on_device(): pl.pallas_call(hand_over, out_shape=(out, out), in_specs=[vmem, vmem], ou...  0.69 us

profile of v2, /device:TPU:0, one launch (start us, length us, event | category | flops | bytes accessed | tf_op | source)
XLA Modules:
  0.0 23.8 jit_solution(11976554263627814914)
XLA Ops:
  1.3 21.9 %shard_map.86 = (bf16[18,2048]{1,0:T(8,128)(2,1)S(1)}, bf16[18,2048]{1,0:T(8,128)(2,1)S(1)}) custom-call(s32[18]{0:T(128)} %lengths.1, s32[1]{0:T(128)S(6)} %copy.9.live, s32[18]{0:T(128)} %index.1, bf16[18,2048]{1,0:T(8,128)(2,1)} %queries.1, bf16[2,18,128,256]{3,2,1,0:T(8,128)(2,1)} %cache.1, bf16[4,16,2048]{2,1,0:T(8,128)(2,1)} %down.1, ...), custom_call_target="tpu_custom_call" | custom-call | tf_op jit(solution)/shard_map/pallas_call | solution.py:361
  23.1 0.7 %shard_map.87 = (bf16[18,2048]{1,0:T(8,128)(2,1)}, bf16[18,2048]{1,0:T(8,128)(2,1)}) custom-call(bf16[18,2048]{1,0:T(8,128)(2,1)S(1)} %get-tuple-element.4.attention, bf16[18,2048]{1,0:T(8,128)(2,1)S(1)} %get-tuple-element.5.adapted), custom_call_target="tpu_custom_call" | custom-call | tf_op jit(solution)/shard_map/pallas_call | solution.py:369
